TPU v7x, 128 devices: a whole 4x4x4 slice. The times are simulated.
128 devices in a mesh: gx: 32 (over z, y, x_hi), gy: 4 (over x_lo, core).
Axes of the slice: x: 4 (x_hi: 2, x_lo: 2; x = x_hi * 2 + x_lo), y: 4, z: 4, core: 2. Of those that a mesh axis runs over, the one named last changes fastest.
Arguments:
- populations: float32 [27, 128, 64, 256], P(None, 'gx', 'gy'), may hold values from 0.4 to 1.6
- omega: float32 [128, 64, 256], P('gx', 'gy'), may hold values from 1.2 to 1.9
- walls: int32 [128, 64, 256], P('gx', 'gy'), may hold values 0 or 1
- radiation: bfloat16 [4096, 512], replicated, may hold values from -0.25 to 0.25
- bins: int32 [512, 32], replicated, may hold values from 0 to 126
- counts: int32 [32, 4], P('gx', 'gy'), may hold values from 1 to 16, as said below
- sample_site: int32 [32, 4, 16], P('gx', 'gy'), may hold values from 0 to 127, as said below
- sample_patch: int32 [32, 4, 16], P('gx', 'gy'), may hold values from 0 to 511, as said below
Outputs:
- advanced: float32 [27, 128, 64, 256], P(None, 'gx', 'gy')
- signal: float32 [4096, 128], P(('gx', 'gy'))
Inputs may be any that keep to these rules, and one draw needn't show every extreme that they name: `counts`: live samples fill a device's first slots; some device has all 16. `sample_site`: site numbers of one device are distinct. `sample_patch`: a device with gy index j names only patches j * 128 to (j + 1) * 128 - 1.
All inputs are finite; a program needn't handle non-finite values. No bound on the sum of `walls` on one device may be relied on, other than what follows from the above.
Results may differ from a plain program's by a relative error of at most 0.0037.
Values may be sent and summed in bfloat16 or wider, within the bound.
A program may use at most 64 MiB of HBM per device.

v0:
```python
import jax
import jax.numpy as jnp
from jax import lax
from jax.sharding import PartitionSpec as P

ZS = 128
PATCH_OWN = 32
OBS = 4096
OBS_BLK = 128
LEVELS = 128
STEPS = 2


def extended(x, sides, width):
    for axis, dim in sides:
        size, length = (lax.axis_size(axis), x.shape[dim])
        up = [(i, (i + 1) % size) for i in range(size)]
        down = [(j, i) for i, j in up]
        last = lax.slice_in_dim(x, length - width, length, axis=dim)
        initial = lax.slice_in_dim(x, 0, width, axis=dim)
        before = lax.ppermute(last, axis, up)
        after = lax.ppermute(initial, axis, down)
        x = jnp.concatenate([before, x, after], axis=dim)
    return x


def lattice_weight():
    values = []
    for direction in range(27):
        moving = int(direction // 9 != 1) + int(direction // 3 % 3 != 1) + int(direction % 3 != 1)
        values.append([8.0 / 27.0, 2.0 / 27.0, 1.0 / 54.0, 1.0 / 216.0][moving])
    return jnp.array(values, dtype=jnp.float32)


def forward(lattice, axis_index, velocity):
    rotated = jnp.moveaxis(lattice, axis_index, 0)
    minus_side, centre, plus_side = (rotated[0], rotated[1], rotated[2])
    summed = minus_side + centre + plus_side
    difference = plus_side - minus_side
    first_order = difference - velocity * summed
    second_order = (
        plus_side + minus_side - 2.0 * velocity * difference + velocity * velocity * summed
    )
    return jnp.moveaxis(jnp.stack([summed, first_order, second_order]), 0, axis_index)


def backward(lattice, axis_index, velocity):
    rotated = jnp.moveaxis(lattice, axis_index, 0)
    order_zero, order_one, order_two = (rotated[0], rotated[1], rotated[2])
    difference = order_one + velocity * order_zero
    summed_ends = order_two + 2.0 * velocity * order_one + velocity * velocity * order_zero
    minus_side = 0.5 * (summed_ends - difference)
    plus_side = 0.5 * (summed_ends + difference)
    centre = order_zero - summed_ends
    return jnp.moveaxis(jnp.stack([minus_side, centre, plus_side]), 0, axis_index)


def collide(distribution, omega):
    trailing = distribution.shape[1:]
    lattice = distribution.reshape((3, 3, 3) + trailing)
    density = jnp.sum(lattice, axis=(0, 1, 2))
    vel_x = jnp.sum(lattice[2] - lattice[0], axis=(0, 1)) / density
    vel_y = jnp.sum(lattice[:, 2] - lattice[:, 0], axis=(0, 1)) / density
    vel_z = jnp.sum(lattice[:, :, 2] - lattice[:, :, 0], axis=(0, 1)) / density
    moments = forward(lattice, 2, vel_z)
    moments = forward(moments, 1, vel_y)
    moments = forward(moments, 0, vel_x)
    retain = 1.0 - omega
    normal_xy = retain * (moments[2, 0, 0] - moments[0, 2, 0])
    normal_xz = retain * (moments[2, 0, 0] - moments[0, 0, 2])
    post_xx = (density + normal_xy + normal_xz) / 3.0
    post_yy = (density - 2.0 * normal_xy + normal_xz) / 3.0
    post_zz = (density + normal_xy - 2.0 * normal_xz) / 3.0
    post_xy = retain * moments[1, 1, 0]
    post_xz = retain * moments[1, 0, 1]
    post_yz = retain * moments[0, 1, 1]
    inverse = 1.0 / density
    entries = {
        (0, 0, 0): density,
        (2, 0, 0): post_xx,
        (0, 2, 0): post_yy,
        (0, 0, 2): post_zz,
        (1, 1, 0): post_xy,
        (1, 0, 1): post_xz,
        (0, 1, 1): post_yz,
        (2, 2, 0): (post_xx * post_yy + 2.0 * post_xy * post_xy) * inverse,
        (2, 0, 2): (post_xx * post_zz + 2.0 * post_xz * post_xz) * inverse,
        (0, 2, 2): (post_yy * post_zz + 2.0 * post_yz * post_yz) * inverse,
        (2, 1, 1): (post_xx * post_yz + 2.0 * post_xy * post_xz) * inverse,
        (1, 2, 1): (post_yy * post_xz + 2.0 * post_xy * post_yz) * inverse,
        (1, 1, 2): (post_zz * post_xy + 2.0 * post_xz * post_yz) * inverse,
        (2, 2, 2): (
            post_xx * post_yy * post_zz
            + 2.0 * post_xx * post_yz * post_yz
            + 2.0 * post_yy * post_xz * post_xz
            + 2.0 * post_zz * post_xy * post_xy
            + 8.0 * post_xy * post_xz * post_yz
        )
        * inverse
        * inverse,
    }
    nothing = jnp.zeros_like(density)
    listed = [
        entries.get((order_x, order_y, order_z), nothing)
        for order_x in range(3)
        for order_y in range(3)
        for order_z in range(3)
    ]
    relaxed = jnp.stack(listed).reshape((3, 3, 3) + trailing)
    relaxed = backward(relaxed, 0, vel_x)
    relaxed = backward(relaxed, 1, vel_y)
    relaxed = backward(relaxed, 2, vel_z)
    return relaxed.reshape((27,) + trailing)


def macro_rows(read):
    lattice = read.reshape((3, 3, 3) + read.shape[1:])
    density = jnp.sum(lattice, axis=(0, 1, 2))
    mom_x = jnp.sum(lattice[2] - lattice[0], axis=(0, 1))
    mom_y = jnp.sum(lattice[:, 2] - lattice[:, 0], axis=(0, 1))
    mom_z = jnp.sum(lattice[:, :, 2] - lattice[:, :, 0], axis=(0, 1))
    return jnp.stack([density - 1.0, mom_x, mom_y, mom_z])


def widen(relaxed):
    return extended(relaxed, (("gx", 1), ("gy", 2)), 1)


def stream(relaxed, padded, before, solid_cell, blocked_rim):
    width_x, width_y = (relaxed.shape[1], relaxed.shape[2])
    gathered = []
    for direction in range(27):
        step_x = direction // 9 - 1
        step_y = direction // 3 % 3 - 1
        step_z = direction % 3 - 1
        source = padded[
            direction, 1 - step_x : 1 - step_x + width_x, 1 - step_y : 1 - step_y + width_y
        ]
        source = jnp.roll(source, step_z, axis=2)
        blocked = blocked_rim[1 - step_x : 1 - step_x + width_x, 1 - step_y : 1 - step_y + width_y]
        blocked = jnp.roll(blocked, step_z, axis=2)
        bounced = jnp.where(blocked, relaxed[26 - direction], source)
        gathered.append(jnp.where(solid_cell, before[direction], bounced))
    return jnp.stack(gathered)


def evaluate(patch_sum, first_patch, step_index, radiation, bins):
    held_patches = patch_sum.shape[0]
    response = lax.dot_general(
        radiation,
        patch_sum.astype(jnp.bfloat16),
        (((1,), (1,)), ((), ())),
        preferred_element_type=jnp.float32,
    )
    delays = lax.dynamic_slice_in_dim(bins, first_patch, held_patches, 0) + step_index
    one_hot = (delays[:, :, None] == jnp.arange(LEVELS, dtype=jnp.int32)).astype(jnp.float32)
    binned = jnp.einsum(
        "bop,pbl->bol",
        response.reshape(OBS // OBS_BLK, OBS_BLK, held_patches),
        one_hot,
        precision=lax.Precision.HIGHEST,
    )
    return binned.reshape(OBS, LEVELS)


def per_device(populations, omega, walls, radiation, bins, counts, sample_site, sample_patch):
    weight = lattice_weight()[:, None, None, None]
    solid_cell = walls == 1
    wall_halo = extended(walls, (("gx", 0), ("gy", 1)), 1)
    blocked_rim = wall_halo == 1
    slot_count = sample_site.shape[-1]
    slot_sites = sample_site.reshape(slot_count)
    live_slot = jnp.arange(slot_count, dtype=jnp.int32) < counts.reshape(())
    column = lax.axis_index("gy")
    row_index = lax.axis_index("gx")
    axis_devices = lax.axis_size("gx")
    column_patches = PATCH_OWN * (axis_devices // 8)
    local_patch = sample_patch.reshape(slot_count) - column * column_patches
    share_rows = column_patches // axis_devices
    safe_patch = jnp.where(live_slot, local_patch, -1)
    signal = jnp.zeros((OBS, LEVELS), jnp.float32)
    current = populations
    for step_index in range(STEPS):
        before = current * weight
        relaxed = collide(before, omega)
        padded = widen(relaxed)
        read = stream(relaxed, padded, before, solid_cell, blocked_rim)
        current = read / weight
        taken_cells = jnp.take(read.reshape(27, -1, ZS), slot_sites, axis=1)
        gathered_rows = jnp.moveaxis(macro_rows(taken_cells), 0, 1).reshape(slot_count, 4 * ZS)
        surface = jnp.where(live_slot[:, None], gathered_rows, 0.0).astype(jnp.bfloat16)
        wanted = jnp.arange(share_rows * lax.axis_size("gx"), dtype=jnp.int32)
        selector = (safe_patch[None, :] == wanted[:, None]).astype(jnp.bfloat16)
        patch_sum = lax.psum_scatter(
            jnp.dot(selector, surface, preferred_element_type=jnp.float32),
            "gx",
            scatter_dimension=0,
            tiled=True,
        )
        first_patch = column * column_patches + row_index * share_rows
        signal = signal + evaluate(patch_sum, first_patch, step_index, radiation, bins)
    return (current, lax.psum_scatter(signal, ("gx", "gy"), scatter_dimension=0, tiled=True))


def solution(mesh):
    return jax.shard_map(
        per_device,
        mesh=mesh,
        in_specs=(
            P(None, "gx", "gy", None),
            P("gx", "gy", None),
            P("gx", "gy", None),
            P(),
            P(),
            P("gx", "gy"),
            P("gx", "gy", None),
            P("gx", "gy", None),
        ),
        out_specs=(P(None, "gx", "gy", None), P(("gx", "gy"), None)),
        check_vma=False,
    )
```

profile of v0, /device:TPU:1, one launch (start us, length us, event | category | flops | bytes accessed | tf_op | source)
XLA Modules:
  0.0 1045.8 jit_solution(778101440038244317)
XLA Ops:
  7.2 1.7 fusion.219
  14.9 3.6 collective-permute-start.4
  18.5 5.9 collective-permute-start.5
  24.4 7.2 collective-permute-start.1
  32.2 11.8 %collective-permute-done = s32[1,16,256]{2,1,0:T(8,128)S(1)} collective-permute-done((s32[1,16,256]{2,1,0:T(8,128)S(1)}, s32[1,16,256]{2,1,0:T(8,128)S(1)}, u32[]{:S(2)}, u32[]{:S(2)}) %collective-permute-start) | collective-permute-done | bytes 16416 | tf_op jit(solution)/shard_map/ppermute | solution.py:21
  45.3 1.9 collective-permute-start.2
  48.4 2.0 collective-permute-done.3
  53.4 1.7 collective-permute-start.7
  55.5 3.9 collective-permute-done.6
  94.2 7.2 collective-permute-start.9
  102.0 8.4 collective-permute-done.8
  110.4 4.3 collective-permute-done.9
  124.5 1.5 stack.589
  133.6 1.5 stack.583
  135.2 1.5 stack.582
  142.8 1.5 stack.577
  150.4 8.0 stack.600
  158.4 2.3 gather_fusion
  197.0 4.4 stack.632
  203.3 164.7 %all-reduce.4 = (bf16[128,512]{1,0:T(8,128)(2,1)S(1)}, bf16[128,512]{1,0:T(8,128)(2,1)S(1)}) all-reduce(f32[128,512]{1,0:T(8,128)S(1)} %fusion.200, f32[128,512]{1,0:T(8,128)S(1)} %fusion.199), channel_id=2, replica_groups=mesh['gx'=32,'gy'=4] {'gx'}, use_global_device_ids=true, to_apply=%region_12.14.clone | all-reduce | flops 131072 | bytes 786432
  368.1 3.5 convolution_bitcast_fusion.1
  372.8 1.9 fusion.201
  374.7 3.2 convolution_add_fusion
  380.8 658.2 %reduce-scatter.2.cloned.1.call-done = f32[32,128]{1,0:T(8,128)} async-done(((f32[4096,128]{1,0:T(8,128)}), f32[32,128]{1,0:T(8,128)}) %reduce-scatter.2.cloned.1.call-update) | async-done | bytes 16400 | tf_op jit(solution)/shard_map/reduce_scatter | solution.py:202
  (540 shorter events, 116.5 us)
Async XLA Ops:
  7.2 1031.8 %reduce-scatter.2.cloned.1.call-start = ((), (), s32[]{:S(2)}) async-start(), calls=%async_computation.1 | async-start | bytes 2113536 | tf_op jit(solution)/shard_map/reduce_scatter | solution.py:202
  14.9 36.9 %collective-permute-start.4 = (f32[27,1,16,256]{3,2,1,0:T(8,128)}, f32[27,1,16,256]{3,2,1,0:T(8,128)}, u32[]{:S(2)}, u32[]{:S(2)}) collective-permute-start(f32[27,1,16,256]{3,2,1,0:T(8,128)} %get-tuple-element.258), channel_id=1, source_target_pairs={{0,4},{4,8},{8,12},{12,16},{16,20},{20,24},{24,28},{28,32},{32,36}... | collective-permute-start | bytes 1327112 | tf_op jit(solution)/shard_map/ppermute | solution.py:21
  18.5 33.4 %collective-permute-start.5 = (f32[27,1,16,256]{3,2,1,0:T(8,128)}, f32[27,1,16,256]{3,2,1,0:T(8,128)}, u32[]{:S(2)}, u32[]{:S(2)}) collective-permute-start(f32[27,1,16,256]{3,2,1,0:T(8,128)} %get-tuple-element.259), channel_id=1, source_target_pairs={{4,0},{8,4},{12,8},{16,12},{20,16},{24,20},{28,24},{32,28},{36,32}... | collective-permute-start | bytes 1327112 | tf_op jit(solution)/shard_map/ppermute | solution.py:22
  24.4 19.6 %collective-permute-start = (s32[1,16,256]{2,1,0:T(8,128)S(1)}, s32[1,16,256]{2,1,0:T(8,128)S(1)}, u32[]{:S(2)}, u32[]{:S(2)}) collective-permute-start(s32[1,16,256]{2,1,0:T(8,128)S(1)} %get-tuple-element.281), channel_id=1, source_target_pairs={{0,4},{4,8},{8,12},{12,16},{16,20},{20,24},{24,28},{28,32},{32,36}... | collective-permute-start | bytes 49160 | tf_op jit(solution)/shard_map/ppermute | solution.py:21
  24.4 19.6 %collective-permute-start.1 = (s32[1,16,256]{2,1,0:T(8,128)S(1)}, s32[1,16,256]{2,1,0:T(8,128)S(1)}, u32[]{:S(2)}, u32[]{:S(2)}) collective-permute-start(s32[1,16,256]{2,1,0:T(8,128)S(1)} %get-tuple-element.280), channel_id=1, source_target_pairs={{4,0},{8,4},{12,8},{16,12},{20,16},{24,20},{28,24},{32,28},{36,32}... | collective-permute-start | bytes 49160 | tf_op jit(solution)/shard_map/ppermute | solution.py:22
  45.3 3.2 collective-permute-start.2
  47.2 3.3 collective-permute-start.3
  51.4 33.0 %copy-start.1 = (pred[6,18,256]{2,1,0:T(8,128)(4,1)}, pred[6,18,256]{2,1,0:T(8,128)(4,1)S(1)}, u32[]{:S(2)}) copy-start(pred[6,18,256]{2,1,0:T(8,128)(4,1)S(1)} %add_compare_fusion) | copy-start | bytes 82948
  51.8 26.1 %copy-start.44 = (pred[4,16,255]{2,1,0:T(8,128)(4,1)}, pred[4,16,255]{2,1,0:T(8,128)(4,1)S(1)}, u32[]{:S(2)}) copy-start(pred[4,16,255]{2,1,0:T(8,128)(4,1)S(1)} %get-tuple-element.311) | copy-start | bytes 48964
  51.8 28.4 %copy-start.42 = (pred[4,16,255]{2,1,0:T(8,128)(4,1)}, pred[4,16,255]{2,1,0:T(8,128)(4,1)S(1)}, u32[]{:S(2)}) copy-start(pred[4,16,255]{2,1,0:T(8,128)(4,1)S(1)} %get-tuple-element.310) | copy-start | bytes 48964
  51.8 29.1 %copy-start.40 = (pred[4,16,255]{2,1,0:T(8,128)(4,1)}, pred[4,16,255]{2,1,0:T(8,128)(4,1)S(1)}, u32[]{:S(2)}) copy-start(pred[4,16,255]{2,1,0:T(8,128)(4,1)S(1)} %get-tuple-element.309) | copy-start | bytes 48964
  51.8 31.2 %copy-start.38 = (pred[4,16,255]{2,1,0:T(8,128)(4,1)}, pred[4,16,255]{2,1,0:T(8,128)(4,1)S(1)}, u32[]{:S(2)}) copy-start(pred[4,16,255]{2,1,0:T(8,128)(4,1)S(1)} %get-tuple-element.308) | copy-start | bytes 48964
  51.8 31.9 %copy-start.36 = (pred[4,16,255]{2,1,0:T(8,128)(4,1)}, pred[4,16,255]{2,1,0:T(8,128)(4,1)S(1)}, u32[]{:S(2)}) copy-start(pred[4,16,255]{2,1,0:T(8,128)(4,1)S(1)} %get-tuple-element.307) | copy-start | bytes 48964
  51.8 34.1 %copy-start.34 = (pred[4,16,255]{2,1,0:T(8,128)(4,1)}, pred[4,16,255]{2,1,0:T(8,128)(4,1)S(1)}, u32[]{:S(2)}) copy-start(pred[4,16,255]{2,1,0:T(8,128)(4,1)S(1)} %get-tuple-element.306) | copy-start | bytes 48964
  53.3 6.0 collective-permute-start.6
  53.4 6.0 collective-permute-start.7
  55.4 27.5 %copy-start.76 = (pred[4,16,1]{2,1,0:T(8,128)(4,1)}, pred[4,16,1]{2,1,0:T(8,128)(4,1)S(1)}, u32[]{:S(2)}) copy-start(pred[4,16,1]{2,1,0:T(8,128)(4,1)S(1)} %get-tuple-element.290) | copy-start | bytes 196
  55.5 28.2 %copy-start.74 = (pred[4,16,1]{2,1,0:T(8,128)(4,1)}, pred[4,16,1]{2,1,0:T(8,128)(4,1)S(1)}, u32[]{:S(2)}) copy-start(pred[4,16,1]{2,1,0:T(8,128)(4,1)S(1)} %get-tuple-element.289) | copy-start | bytes 196
  55.5 30.5 %copy-start.72 = (pred[4,16,1]{2,1,0:T(8,128)(4,1)}, pred[4,16,1]{2,1,0:T(8,128)(4,1)S(1)}, u32[]{:S(2)}) copy-start(pred[4,16,1]{2,1,0:T(8,128)(4,1)S(1)} %get-tuple-element.288) | copy-start | bytes 196
  94.1 26.0 %copy-start.15 = (f32[4,16,256]{2,1,0:T(8,128)S(1)}, f32[4,16,256]{2,1,0:T(8,128)}, u32[]{:S(2)}) copy-start(f32[4,16,256]{2,1,0:T(8,128)} %get-tuple-element.106) | copy-start | bytes 196612
  94.1 16.3 %collective-permute-start.8 = (f32[27,1,16,256]{3,2,1,0:T(8,128)S(1)}, f32[27,1,16,256]{3,2,1,0:T(8,128)S(1)}, u32[]{:S(2)}, u32[]{:S(2)}) collective-permute-start(f32[27,1,16,256]{3,2,1,0:T(8,128)S(1)} %get-tuple-element.252), channel_id=1, source_target_pairs={{0,4},{4,8},{8,12},{12,16},{16,20},{20,24},{24,28},{28,32},{32,36}... | collective-permute-start | bytes 1327112 | tf_op jit(solution)/shard_map/ppermute | solution.py:21
  94.2 20.4 %collective-permute-start.9 = (f32[27,1,16,256]{3,2,1,0:T(8,128)S(1)}, f32[27,1,16,256]{3,2,1,0:T(8,128)S(1)}, u32[]{:S(2)}, u32[]{:S(2)}) collective-permute-start(f32[27,1,16,256]{3,2,1,0:T(8,128)S(1)} %get-tuple-element.253), channel_id=1, source_target_pairs={{4,0},{8,4},{12,8},{16,12},{20,16},{24,20},{28,24},{32,28},{36,32}... | collective-permute-start | bytes 1327112 | tf_op jit(solution)/shard_map/ppermute | solution.py:22
  115.6 45.1 %collective-permute-start.10 = (f32[27,6,1,256]{3,2,1,0:T(1,128)}, f32[27,6,1,256]{3,2,1,0:T(1,128)S(1)}, u32[]{:S(2)}, u32[]{:S(2)}) collective-permute-start(f32[27,6,1,256]{3,2,1,0:T(1,128)} %get-tuple-element.225), channel_id=1, source_target_pairs={{1,0},{2,1},{3,2},{0,3},{5,4},{6,5},{7,6},{4,7},{9,8},{10,9},{11,1... | collective-permute-start | bytes 497672 | tf_op jit(solution)/shard_map/ppermute | solution.py:22
  116.9 43.9 %collective-permute-start.11 = (f32[27,6,1,256]{3,2,1,0:T(1,128)}, f32[27,6,1,256]{3,2,1,0:T(1,128)S(1)}, u32[]{:S(2)}, u32[]{:S(2)}) collective-permute-start(f32[27,6,1,256]{3,2,1,0:T(1,128)} %get-tuple-element.224), channel_id=1, source_target_pairs={{0,1},{1,2},{2,3},{3,0},{4,5},{5,6},{6,7},{7,4},{8,9},{9,10},{10,1... | collective-permute-start | bytes 497672 | tf_op jit(solution)/shard_map/ppermute | solution.py:21
  (106 other events, 907.3 us)
Sparse Core Ops, SparseCore 0:
  378.1 660.8 reduce-scatter.1
where the time goes:
time: 1050 us
  waiting for transfers between devices  689 us (66%)
  blocking collectives  165 us (16%)
  local copies, waits for them, and re-layouts  74.9 us (7%)
  other arithmetic  60.5 us (6%)
  starting transfers between devices  29.4 us (3%)
  between operations  17.4 us (2%)
    reduce_scatter x1, waiting for transfers between devices, per_device(): lax.psum_scatter(signal, ('gx', 'gy'), scatter_dimension=0, tiled=True)  658 us
    unnamed x1, blocking collectives  165 us
    another operation x56, local copies, waits for them, and re-layouts, stream(): return jnp.stack(gathered)  58.3 us
    unnamed x62, other arithmetic  32.6 us
    ppermute x6, starting transfers between devices, extended(): after = lax.ppermute(initial, axis, down)  21.6 us
  transfers between devices with their start and end apart: 13, of which 6 were waited for; matrix products, arithmetic and copies ran while one was open for 5% of the time, Pallas kernels for 0%

commit v1 on v0

v1 whole, which is shorter than its diff:
```python
import functools

import jax
import jax.numpy as jnp
from jax import lax
from jax.experimental import pallas as pl
from jax.experimental.pallas import tpu as pltpu
from jax.sharding import PartitionSpec as P

CX = 4
CY = 16
NZ = 256
ZS = 128
SAMP = 16
LEVELS = 128
COLUMN = 128
OWN = 32
WALL = 2.0**100
WALL_TEST = 2.0**60
MESH = pl.DeviceIdType.MESH
F32 = jnp.float32
BF16 = jnp.bfloat16
CORNERS = ((-1, -1), (-1, 1), (1, -1), (1, 1))


def moments(g):
    def pair(lo, hi):
        return lo + hi, hi - lo

    s0 = [[None] * 3 for _ in range(3)]
    s1 = [[None] * 3 for _ in range(3)]
    s2 = [[None] * 3 for _ in range(3)]
    for a in range(3):
        for b in range(3):
            lo, mid, hi = g(a, b, 0), g(a, b, 1), g(a, b, 2)
            s2[a][b], s1[a][b] = pair(lo, hi)
            s0[a][b] = 4.0 * mid + s2[a][b]
    t00, t10, t20, t01, t11, t02 = [], [], [], [], [], []
    for a in range(3):
        ends, gap = pair(s0[a][0], s0[a][2])
        t00.append(4.0 * s0[a][1] + ends)
        t10.append(gap)
        t20.append(ends)
        ends, gap = pair(s1[a][0], s1[a][2])
        t01.append(4.0 * s1[a][1] + ends)
        t11.append(gap)
        t02.append(4.0 * s2[a][1] + (s2[a][0] + s2[a][2]))

    def whole(t):
        return 4.0 * t[1] + (t[0] + t[2])

    m200 = t00[0] + t00[2]
    return {
        "000": 4.0 * t00[1] + m200,
        "100": t00[2] - t00[0],
        "200": m200,
        "010": whole(t10),
        "110": t10[2] - t10[0],
        "020": whole(t20),
        "001": whole(t01),
        "101": t01[2] - t01[0],
        "011": whole(t11),
        "002": whole(t02),
    }


def line(o0, o1, o2, v):
    if o1 is None:
        d = v * o0
        e = o2 + v * d
    else:
        d = o1 + v * o0
        e = o2 + v * (o1 + d)
    return e - d, 0.5 * (o0 - e), e + d


def odd_line(o1, v):
    c = v * o1
    e = c + c
    return e - o1, -c, e + o1


def collided(m, omega):
    inv_m = 1.0 / m["000"]
    ux, uy, uz = m["100"] * inv_m, m["010"] * inv_m, m["001"] * inv_m
    n = {k: 0.125 * v for k, v in m.items()}
    rho, mx, my, mz = n["000"], n["100"], n["010"], n["001"]
    inverse = 8.0 * inv_m
    retain = 1.0 - omega
    c200 = n["200"] - mx * ux
    c020 = n["020"] - my * uy
    c002 = n["002"] - mz * uz
    third = 1.0 / 3.0
    d1 = retain * (c200 - c020)
    d2 = retain * (c200 - c002)
    total = rho + d1 + d2
    kxx = total * third
    kyy = (total - 3.0 * d1) * third
    kzz = (total - 3.0 * d2) * third
    kxy = retain * (n["110"] - mx * uy)
    kxz = retain * (n["101"] - mx * uz)
    kyz = retain * (n["011"] - my * uz)
    sxy, sxz, syz = kxy * kxy, kxz * kxz, kyz * kyz
    xy_xz, xy_yz, xz_yz = kxy * kxz, kxy * kyz, kxz * kyz
    k220 = (kxx * kyy + 2.0 * sxy) * inverse
    k202 = (kxx * kzz + 2.0 * sxz) * inverse
    yy_zz = kyy * kzz
    k022 = (yy_zz + 2.0 * syz) * inverse
    k211 = (kxx * kyz + 2.0 * xy_xz) * inverse
    k121 = (kyy * kxz + 2.0 * xy_yz) * inverse
    k112 = (kzz * kxy + 2.0 * xz_yz) * inverse
    k222 = (
        kxx * (yy_zz + 2.0 * syz) + 2.0 * (kyy * sxz + kzz * sxy) + 8.0 * (kxy * xz_yz)
    ) * (inverse * inverse)
    cols = {
        (0, 0): line(rho, None, kxx, ux),
        (1, 0): odd_line(kxy, ux),
        (2, 0): line(kyy, None, k220, ux),
        (0, 1): odd_line(kxz, ux),
        (1, 1): line(kyz, None, k211, ux),
        (2, 1): odd_line(k121, ux),
        (0, 2): line(kzz, None, k202, ux),
        (1, 2): odd_line(k112, ux),
        (2, 2): line(k022, None, k222, ux),
    }
    for a in range(3):
        by_y = [line(cols[0, c][a], cols[1, c][a], cols[2, c][a], uy) for c in range(3)]
        for b in range(3):
            ends = line(by_y[0][b], by_y[1][b], by_y[2][b], uz)
            for c in range(3):
                yield 9 * a + 3 * b + c, ends[c]


def kernel(
    n_gx,
    n_gy,
    count_ref,
    site_ref,
    patch_ref,
    pop_hbm,
    omega_hbm,
    walls_hbm,
    rad_hbm,
    bins_hbm,
    adv_hbm,
    sig_ref,
    f_ref,
    rel,
    omega,
    walls,
    rad,
    bins,
    xsend,
    xrecv,
    ysend,
    yrecv,
    csend,
    crecv,
    lv_own,
    lv_gy,
    lv_sum,
    lv_in,
    one_hot,
    fields,
    rows,
    resp,
    resp_in,
    load_sem,
    out_sem,
    halo_send,
    halo_recv,
    lvg_send,
    lvg_recv,
    lva_send,
    lva_recv,
    row_send,
    row_recv,
    resp_send,
    resp_recv,
):
    me_x, me_y = lax.axis_index("gx"), lax.axis_index("gy")

    def at_x(d):
        return lax.rem(me_x + (d + n_gx), n_gx)

    def at_y(d):
        return lax.rem(me_y + (d + n_gy), n_gy)

    layers = (0, 3, 1, 2)
    pop_loads = [
        pltpu.make_async_copy(pop_hbm.at[:, x], f_ref.at[:, x], load_sem.at[x]) for x in range(CX)
    ]
    omega_load = pltpu.make_async_copy(omega_hbm, omega, load_sem.at[4])
    walls_load = pltpu.make_async_copy(walls_hbm, walls, load_sem.at[5])
    bins_load = pltpu.make_async_copy(
        bins_hbm.at[pl.ds(pl.multiple_of(me_y * COLUMN, COLUMN), COLUMN)], bins, load_sem.at[6]
    )
    rad_load = pltpu.make_async_copy(rad_hbm.at[:, me_y], rad, load_sem.at[7])
    bins_load.start()
    omega_load.start()
    walls_load.start()
    for x in layers:
        pop_loads[x].start()
    rad_load.start()

    barrier = pltpu.get_barrier_semaphore()

    @pl.loop(1, n_gx)
    def _(d):
        pl.semaphore_signal(barrier, inc=1, device_id=(at_x(d), me_y), device_id_type=MESH)

    for e in range(1, n_gy):
        pl.semaphore_signal(barrier, inc=1, device_id=(me_x, at_y(e)), device_id_type=MESH)
    for sx, sy in CORNERS:
        pl.semaphore_signal(barrier, inc=1, device_id=(at_x(sx), at_y(sy)), device_id_type=MESH)

    lane = lax.broadcasted_iota(jnp.int32, (COLUMN, 128), 1)
    sub = lax.broadcasted_iota(jnp.int32, (COLUMN, 128), 0)
    slot_patch = jnp.full((COLUMN, 128), -1, jnp.int32)
    for k in range(SAMP):
        local = patch_ref[0, k] - me_y * COLUMN
        slot_patch = jnp.where(lane % 64 == me_y * SAMP + k, local, slot_patch)
    pick = (slot_patch == sub).astype(BF16)
    bins_load.wait()
    level = lax.dot_general(
        bins[...].astype(F32).astype(BF16), pick, (((0,), (0,)), ((), ())), preferred_element_type=F32
    )
    lane_b = lax.broadcasted_iota(jnp.int32, (n_gx, 128), 1)
    later = (lane_b >= 64) & ((lane_b % 64) // SAMP == me_y)
    level = level + jnp.where(later, 1.0, 0.0)
    for b in range(n_gx):
        lv_own[b] = level[b : b + 1, :]

    sub_k = lax.broadcasted_iota(jnp.int32, (SAMP, 128), 0)
    lane_k = lax.broadcasted_iota(jnp.int32, (SAMP, 128), 1)
    target = jnp.full((SAMP, 128), -1, jnp.int32)
    for k in range(SAMP):
        site = site_ref[0, k]
        target = jnp.where(sub_k == k, (site % 2) * 64 + site // 2, target)
    live = (target == lane_k) & (sub_k < count_ref[0, 0])
    selector = live.astype(BF16)

    def collide(first, step, with_fields):
        @pl.loop(0, 8)
        def _(j):
            x = first + (j // 4) * step
            y0 = pl.multiple_of(((j // 2) % 2) * 8, 8)
            z0 = pl.multiple_of((j % 2) * 128, 128)

            def g(a, b, c):
                return f_ref[9 * a + 3 * b + c, x, pl.ds(y0, 8), pl.ds(z0, 128)]

            m = moments(g)
            solid = walls[x, pl.ds(y0, 8), pl.ds(z0, 128)] == 1
            if with_fields:
                put_fields(m, x, y0, j % 2)
            for i, value in collided(m, omega[x, pl.ds(y0, 8), pl.ds(z0, 128)]):
                rel[i, x + 1, pl.ds(y0 + 8, 8), pl.ds(z0, 128)] = jnp.where(solid, WALL, value)

    def put_fields(m, x, y0, half):
        row = pl.multiple_of(half * 64 + x * CY + y0, 8)
        scale = 1.0 / 216.0
        fields[0, pl.ds(row, 8), :] = m["000"] * scale - 1.0
        fields[1, pl.ds(row, 8), :] = m["100"] * scale
        fields[2, pl.ds(row, 8), :] = m["010"] * scale
        fields[3, pl.ds(row, 8), :] = m["001"] * scale

    def x_copy(s, side):
        sx = 2 * side - 1
        return pltpu.make_async_remote_copy(
            src_ref=xsend.at[s, side],
            dst_ref=xrecv.at[s, side],
            send_sem=halo_send.at[s, side],
            recv_sem=halo_recv.at[s, side],
            device_id=(at_x(sx), me_y),
            device_id_type=MESH,
        )

    def y_copy(s, side):
        sy = 2 * side - 1
        return pltpu.make_async_remote_copy(
            src_ref=ysend.at[s, side],
            dst_ref=yrecv.at[s, side],
            send_sem=halo_send.at[s, 2 + side],
            recv_sem=halo_recv.at[s, 2 + side],
            device_id=(me_x, at_y(sy)),
            device_id_type=MESH,
        )

    def c_copy(s, corner):
        sx, sy = CORNERS[corner]
        return pltpu.make_async_remote_copy(
            src_ref=csend.at[s, corner],
            dst_ref=crecv.at[s, corner],
            send_sem=halo_send.at[s, 4 + corner],
            recv_sem=halo_recv.at[s, 4 + corner],
            device_id=(at_x(sx), at_y(sy)),
            device_id_type=MESH,
        )

    def crossing(sy):
        return [9 * a + 3 * (sy + 1) + c for a in range(3) for c in range(3)]

    def send_x(s):
        for side in range(2):
            for j in range(9):
                value = rel[18 * side + j, 1 + 3 * side, pl.ds(8, CY), :]
                xsend[s, side, j] = (value - 1.0).astype(BF16)
            x_copy(s, side).start()

    def send_y(s):
        for side in range(2):
            edge = 8 + 15 * side
            for j, i in enumerate(crossing(2 * side - 1)):
                for x in range(CX):
                    ysend[s, side, 4 * j + x : 4 * j + x + 1, :] = rel[i, x + 1, edge : edge + 1, :]
            y_copy(s, side).start()
        for corner, (sx, sy) in enumerate(CORNERS):
            edge = 23 if sy > 0 else 8
            x = 4 if sx > 0 else 1
            for c in range(3):
                i = 9 * (sx + 1) + 3 * (sy + 1) + c
                csend[s, corner, c : c + 1, :] = rel[i, x, edge : edge + 1, :]
            c_copy(s, corner).start()

    def take_halo(s):
        for side in range(2):
            y_copy(s, side).wait()
            edge = 7 if side == 1 else 24
            for j, i in enumerate(crossing(2 * side - 1)):
                for x in range(CX):
                    rel[i, x + 1, edge : edge + 1, :] = yrecv[s, side, 4 * j + x : 4 * j + x + 1, :]
        for corner, (sx, sy) in enumerate(CORNERS):
            c_copy(s, corner).wait()
            edge = 7 if sy > 0 else 24
            x = 0 if sx > 0 else 5
            for c in range(3):
                i = 9 * (sx + 1) + 3 * (sy + 1) + c
                rel[i, x, edge : edge + 1, :] = crecv[s, corner, c : c + 1, :]
        for side in range(2):
            x_copy(s, side).wait()
            for j in range(9):
                rel[18 * side + j, 5 - 5 * side, pl.ds(8, CY), :] = (
                    xrecv[s, side, j].astype(F32) + 1.0
                )

    def stream():
        @pl.loop(0, CX)
        def _(x):
            solid = walls[x] == 1
            for i in range(27):
                cx, cy, cz = i // 9 - 1, (i // 3) % 3 - 1, i % 3 - 1
                source = rel[i, x + 1 - cx, pl.ds(8 - cy, CY), :]
                if cz:
                    source = pltpu.roll(source, cz % NZ, 1)
                bounced = jnp.where(
                    source > WALL_TEST, rel[26 - i, x + 1, pl.ds(8, CY), :], source
                )
                f_ref[i, x] = jnp.where(solid, f_ref[i, x], bounced)

    def send_rows(s):
        for part in range(4):
            taken = jnp.dot(selector, fields[part].astype(BF16), preferred_element_type=F32)
            rows[s, me_y, :, part * ZS : (part + 1) * ZS] = taken.astype(BF16)
        for e in range(1, n_gy):
            row_copy(s, e).start()

    def row_copy(s, e):
        return pltpu.make_async_remote_copy(
            src_ref=rows.at[s, me_y],
            dst_ref=rows.at[s, me_y],
            send_sem=row_send.at[s, e],
            recv_sem=row_recv.at[s, e],
            device_id=(me_x, at_y(e)),
            device_id_type=MESH,
        )

    def take_rows(s):
        for e in range(1, n_gy):
            pltpu.make_async_remote_copy(
                src_ref=rows.at[s, me_y],
                dst_ref=rows.at[s, at_y(-e)],
                send_sem=row_send.at[s, e],
                recv_sem=row_recv.at[s, e],
                device_id=(me_x, at_y(e)),
                device_id_type=MESH,
            ).wait()

    def lvg_copy(e):
        return pltpu.make_async_remote_copy(
            src_ref=lv_own,
            dst_ref=lv_gy.at[e],
            send_sem=lvg_send.at[e],
            recv_sem=lvg_recv.at[e],
            device_id=(me_x, at_y(e)),
            device_id_type=MESH,
        )

    def lva_copy(d):
        return pltpu.make_async_remote_copy(
            src_ref=lv_sum.at[at_x(d)],
            dst_ref=lv_in.at[d],
            send_sem=lva_send.at[d],
            recv_sem=lva_recv.at[d],
            device_id=(at_x(d), me_y),
            device_id_type=MESH,
        )

    def resp_copy(d):
        return pltpu.make_async_remote_copy(
            src_ref=resp.at[at_x(d)],
            dst_ref=resp_in.at[d],
            send_sem=resp_send.at[d],
            recv_sem=resp_recv.at[d],
            device_id=(at_x(d), me_y),
            device_id_type=MESH,
        )

    omega_load.wait()
    walls_load.wait()
    pop_loads[0].wait()
    pop_loads[3].wait()
    collide(0, 3, False)
    pl.semaphore_wait(barrier, n_gx - 1 + n_gy - 1 + 4)
    send_x(0)
    for e in range(1, n_gy):
        lvg_copy(e).start()
    pop_loads[1].wait()
    pop_loads[2].wait()
    collide(1, 1, False)
    send_y(0)

    summed = lv_own[...]
    for e in range(1, n_gy):
        lvg_copy(e).wait()
        summed = summed + lv_gy[e]
    lv_sum[...] = summed

    @pl.loop(1, n_gx)
    def _(d):
        lva_copy(d).start()

    lv_in[0] = lv_sum[me_x]
    take_halo(0)
    stream()

    collide(0, 3, True)
    send_x(1)
    collide(1, 1, True)
    send_y(1)
    send_rows(0)

    @pl.loop(0, n_gx)
    def _(d):
        @pl.when(d > 0)
        def _():
            lva_copy(d).wait()

        wanted = lax.broadcasted_iota(jnp.int32, (LEVELS, 128), 0).astype(F32)
        one_hot[d] = (jnp.broadcast_to(lv_in[d], (LEVELS, 128)) == wanted).astype(BF16)

    take_rows(0)
    rad_load.wait()
    take_halo(1)
    stream()
    out_copy = pltpu.make_async_copy(f_ref, adv_hbm, out_sem)
    out_copy.start()

    @pl.loop(0, 16)
    def _(j):
        x = j // 4
        y0 = pl.multiple_of(((j // 2) % 2) * 8, 8)
        z0 = pl.multiple_of((j % 2) * 128, 128)

        def g(a, b, c):
            return f_ref[9 * a + 3 * b + c, x, pl.ds(y0, 8), pl.ds(z0, 128)]

        put_fields(moments(g), x, y0, j % 2)

    send_rows(1)
    take_rows(1)
    all_rows = rows[...].reshape(2 * n_gy * SAMP, 4 * ZS)

    @pl.loop(0, n_gx // 4)
    def _(t):
        block = rad[pl.ds(t * 4, 4)].reshape(4 * OWN, 4 * ZS)
        seen = lax.dot_general(block, all_rows, (((1,), (1,)), ((), ())), preferred_element_type=F32)
        resp[pl.ds(t * 4, 4)] = seen.astype(BF16).reshape(4, OWN, 128)

    @pl.loop(1, n_gx)
    def _(d):
        resp_copy(d).start()

    resp_in[0] = resp[me_x]

    def add(d, total):
        @pl.when(d > 0)
        def _():
            resp_copy(d).wait()

        return total + lax.dot_general(
            resp_in[d], one_hot[d], (((1,), (1,)), ((), ())), preferred_element_type=F32
        )

    sig_ref[...] = lax.fori_loop(0, n_gx, add, jnp.zeros((OWN, LEVELS), F32))
    out_copy.wait()


def per_device(populations, omega, walls, radiation, bins, counts, sample_site, sample_patch):
    n_gx, n_gy = lax.axis_size("gx"), lax.axis_size("gy")
    hbm = pl.BlockSpec(memory_space=pl.ANY)
    smem = pl.BlockSpec(memory_space=pltpu.SMEM)
    vmem = pl.BlockSpec(memory_space=pltpu.VMEM)
    dma = pltpu.SemaphoreType.DMA
    scratch = [
        pltpu.VMEM((27, CX, CY, NZ), F32),
        pltpu.VMEM((27, CX + 2, CY + 16, NZ), F32),
        pltpu.VMEM((CX, CY, NZ), F32),
        pltpu.VMEM((CX, CY, NZ), jnp.int32),
        pltpu.VMEM((n_gx, OWN, 4 * ZS), BF16),
        pltpu.VMEM((COLUMN, n_gx), jnp.int32),
        pltpu.VMEM((2, 2, 9, CY, NZ), BF16),
        pltpu.VMEM((2, 2, 9, CY, NZ), BF16),
        pltpu.VMEM((2, 2, 40, NZ), F32),
        pltpu.VMEM((2, 2, 40, NZ), F32),
        pltpu.VMEM((2, 4, 8, NZ), F32),
        pltpu.VMEM((2, 4, 8, NZ), F32),
        pltpu.VMEM((n_gx, 1, 128), F32),
        pltpu.VMEM((n_gy, n_gx, 1, 128), F32),
        pltpu.VMEM((n_gx, 1, 128), F32),
        pltpu.VMEM((n_gx, 1, 128), F32),
        pltpu.VMEM((n_gx, LEVELS, 128), BF16),
        pltpu.VMEM((4, 128, ZS), F32),
        pltpu.VMEM((2, n_gy, SAMP, 4 * ZS), BF16),
        pltpu.VMEM((n_gx, OWN, 128), BF16),
        pltpu.VMEM((n_gx, OWN, 128), BF16),
        dma((8,)),
        dma,
        dma((2, 8)),
        dma((2, 8)),
        dma((n_gy,)),
        dma((n_gy,)),
        dma((n_gx,)),
        dma((n_gx,)),
        dma((2, n_gy)),
        dma((2, n_gy)),
        dma((n_gx,)),
        dma((n_gx,)),
    ]
    return pl.pallas_call(
        functools.partial(kernel, n_gx, n_gy),
        out_shape=(
            jax.ShapeDtypeStruct((27, CX, CY, NZ), F32),
            jax.ShapeDtypeStruct((OWN, LEVELS), F32),
        ),
        in_specs=[smem] * 3 + [hbm] * 5,
        out_specs=(hbm, vmem),
        scratch_shapes=scratch,
        compiler_params=pltpu.CompilerParams(collective_id=0, has_side_effects=True),
        name="lattice_far_field",
    )(
        counts,
        sample_site.reshape(1, SAMP),
        sample_patch.reshape(1, SAMP),
        populations,
        omega,
        walls,
        radiation.reshape(n_gx, n_gy, OWN, 4 * ZS),
        bins,
    )


def solution(mesh):
    return jax.shard_map(
        per_device,
        mesh=mesh,
        in_specs=(
            P(None, "gx", "gy", None),
            P("gx", "gy", None),
            P("gx", "gy", None),
            P(),
            P(),
            P("gx", "gy"),
            P("gx", "gy", None),
            P("gx", "gy", None),
        ),
        out_specs=(P(None, "gx", "gy", None), P(("gx", "gy"), None)),
        check_vma=False,
    )
```

time: 1050 us -> 53.3 us (0.05)
  waiting for transfers between devices: 689 us -> 0 us
  blocking collectives: 165 us -> 0 us
  local copies, waits for them, and re-layouts: 74.9 us -> 5.2 us
  other arithmetic: 60.5 us -> 0 us
  Pallas kernels: 0 us -> 46.6 us
  starting transfers between devices: 29.4 us -> 0 us
  between operations: 17.4 us -> 1.29 us
    reduce_scatter x1 -> x0, waiting for transfers between devices: 658 us -> none  [per_device(): lax.psum_scatter(signal, ('gx', 'gy'), scatter_dimension=0, tiled=True)]
    unnamed x1 -> x0, blocking collectives: 165 us -> none
    another operation x58 -> x0, local copies, waits for them, and re-layouts: 58.3 us -> none  [the longest x56 58.3 us: stream(): return jnp.stack(gathered)]
    pallas_call x0 -> x1, Pallas kernels: none -> 46.6 us  [per_device(): pl.pallas_call(functools.partial(kernel, n_gx, n_gy), out_shape=(jax.Shap...]
    unnamed x62 -> x0, other arithmetic: 32.6 us -> none
    ppermute x12 -> x0, waiting for transfers between devices: 30.4 us -> none  [the longest x6 20.2 us: extended(): before = lax.ppermute(last, axis, up)]
    ppermute x12 -> x0, starting transfers between devices: 29.4 us -> none  [the longest x6 21.6 us: extended(): after = lax.ppermute(initial, axis, down)]
  transfers between devices with their start and end apart: 13 -> 0, of which waited for: 6 -> 0; matrix products, arithmetic and copies ran while one was open for 5% -> 0% of each run, Pallas kernels for 0% -> 0%
where the time goes in v1:
time: 53.3 us; the launch traced here: 53.1 us
  Pallas kernels  46.6 us (87%)
  local copies, waits for them, and re-layouts  5.2 us (10%)
  between operations  1.29 us (2%)
    pallas_call x1, Pallas kernels, per_device(): pl.pallas_call(functools.partial(kernel, n_gx, n_gy), out_shape=(jax.Shap...  46.6 us
    unnamed x5, local copies, waits for them, and re-layouts  5.2 us

profile of v1, /device:TPU:1, one launch (start us, length us, event | category | flops | bytes accessed | tf_op | source)
XLA Modules:
  0.0 53.1 jit_solution(16672902317221548442)
XLA Ops:
  1.3 1.7 %copy.10.bins_hbm = s32[512,32]{1,0:T(8,128)} copy(s32[512,32]{0,1:T(8,128)} %param.12) | data formatting | bytes 131072 | tf_op args[4]
  3.0 46.6 %lattice_far_field.1 = (f32[27,4,16,256]{3,2,1,0:T(8,128)}, f32[32,128]{1,0:T(8,128)}) custom-call(s32[1,1]{1,0:T(1,128)S(6)} %copy.13.count_ref, s32[1,16]{1,0:T(1,128)} %bitcast.4, s32[1,16]{1,0:T(1,128)} %bitcast.5, f32[27,4,16,256]{3,2,1,0:T(8,128)} %pop_hbm.1, f32[4,16,256]{2,1,0:T(8,128)} %omega_hbm.1, s32[4,16,256]{2,1,0:T(8,128)} %walls_hbm.1, ...), custom_call_target="tpu_custom_call" | custom-call | tf_op jit(solution)/shard_map/lattice_far_field/pallas_call | solution.py:550
  49.5 0.0 copy-start
  49.5 2.9 %copy.14 = f32[27,4,16,256]{3,2,1,0:T(8,128)} copy(f32[27,4,16,256]{3,2,1,0:T(8,128)} %get-tuple-element.4) | data formatting | bytes 3538944
  52.5 0.0 copy-done
  52.5 0.6 %copy.15 = f32[32,128]{1,0:T(8,128)} copy(f32[32,128]{1,0:T(8,128)S(1)} %copy-done) | data formatting | bytes 32768
Async XLA Ops:
  49.5 2.9 %copy-start = (f32[32,128]{1,0:T(8,128)S(1)}, f32[32,128]{1,0:T(8,128)}, u32[]{:S(2)}) copy-start(f32[32,128]{1,0:T(8,128)} %get-tuple-element.5) | copy-start | bytes 49156

commit v2 on v1

--- a/solution.py
+++ b/solution.py
@@ -142,7 +142,7 @@
     walls_hbm,
     rad_hbm,
     bins_hbm,
-    adv_hbm,
+    adv_ref,
     sig_ref,
     f_ref,
     rel,
@@ -166,7 +166,6 @@
     resp,
     resp_in,
     load_sem,
-    out_sem,
     halo_send,
     halo_recv,
     lvg_send,
@@ -193,7 +192,7 @@
     omega_load = pltpu.make_async_copy(omega_hbm, omega, load_sem.at[4])
     walls_load = pltpu.make_async_copy(walls_hbm, walls, load_sem.at[5])
     bins_load = pltpu.make_async_copy(
-        bins_hbm.at[pl.ds(pl.multiple_of(me_y * COLUMN, COLUMN), COLUMN)], bins, load_sem.at[6]
+        bins_hbm.at[:, pl.ds(pl.multiple_of(me_y * COLUMN, COLUMN), COLUMN)], bins, load_sem.at[6]
     )
     rad_load = pltpu.make_async_copy(rad_hbm.at[:, me_y], rad, load_sem.at[7])
     bins_load.start()
@@ -213,32 +212,6 @@
         pl.semaphore_signal(barrier, inc=1, device_id=(me_x, at_y(e)), device_id_type=MESH)
     for sx, sy in CORNERS:
         pl.semaphore_signal(barrier, inc=1, device_id=(at_x(sx), at_y(sy)), device_id_type=MESH)
-
-    lane = lax.broadcasted_iota(jnp.int32, (COLUMN, 128), 1)
-    sub = lax.broadcasted_iota(jnp.int32, (COLUMN, 128), 0)
-    slot_patch = jnp.full((COLUMN, 128), -1, jnp.int32)
-    for k in range(SAMP):
-        local = patch_ref[0, k] - me_y * COLUMN
-        slot_patch = jnp.where(lane % 64 == me_y * SAMP + k, local, slot_patch)
-    pick = (slot_patch == sub).astype(BF16)
-    bins_load.wait()
-    level = lax.dot_general(
-        bins[...].astype(F32).astype(BF16), pick, (((0,), (0,)), ((), ())), preferred_element_type=F32
-    )
-    lane_b = lax.broadcasted_iota(jnp.int32, (n_gx, 128), 1)
-    later = (lane_b >= 64) & ((lane_b % 64) // SAMP == me_y)
-    level = level + jnp.where(later, 1.0, 0.0)
-    for b in range(n_gx):
-        lv_own[b] = level[b : b + 1, :]
-
-    sub_k = lax.broadcasted_iota(jnp.int32, (SAMP, 128), 0)
-    lane_k = lax.broadcasted_iota(jnp.int32, (SAMP, 128), 1)
-    target = jnp.full((SAMP, 128), -1, jnp.int32)
-    for k in range(SAMP):
-        site = site_ref[0, k]
-        target = jnp.where(sub_k == k, (site % 2) * 64 + site // 2, target)
-    live = (target == lane_k) & (sub_k < count_ref[0, 0])
-    selector = live.astype(BF16)
 
     def collide(first, step, with_fields):
         @pl.loop(0, 8)
@@ -344,7 +317,7 @@
                     xrecv[s, side, j].astype(F32) + 1.0
                 )
 
-    def stream():
+    def stream(to_ref):
         @pl.loop(0, CX)
         def _(x):
             solid = walls[x] == 1
@@ -356,7 +329,7 @@
                 bounced = jnp.where(
                     source > WALL_TEST, rel[26 - i, x + 1, pl.ds(8, CY), :], source
                 )
-                f_ref[i, x] = jnp.where(solid, f_ref[i, x], bounced)
+                to_ref[i, x] = jnp.where(solid, f_ref[i, x], bounced)
 
     def send_rows(s):
         for part in range(4):
@@ -423,12 +396,38 @@
     collide(0, 3, False)
     pl.semaphore_wait(barrier, n_gx - 1 + n_gy - 1 + 4)
     send_x(0)
-    for e in range(1, n_gy):
-        lvg_copy(e).start()
     pop_loads[1].wait()
     pop_loads[2].wait()
     collide(1, 1, False)
     send_y(0)
+
+    lane = lax.broadcasted_iota(jnp.int32, (COLUMN, 128), 1)
+    sub = lax.broadcasted_iota(jnp.int32, (COLUMN, 128), 0)
+    slot_patch = jnp.full((COLUMN, 128), -1, jnp.int32)
+    for k in range(SAMP):
+        local = patch_ref[0, k] - me_y * COLUMN
+        slot_patch = jnp.where(lane % 64 == me_y * SAMP + k, local, slot_patch)
+    pick = (slot_patch == sub).astype(BF16)
+    bins_load.wait()
+    level = lax.dot_general(
+        bins[...].astype(F32).astype(BF16), pick, (((1,), (0,)), ((), ())), preferred_element_type=F32
+    )
+    lane_b = lax.broadcasted_iota(jnp.int32, (n_gx, 128), 1)
+    later = (lane_b >= 64) & ((lane_b % 64) // SAMP == me_y)
+    level = level + jnp.where(later, 1.0, 0.0)
+    for b in range(n_gx):
+        lv_own[b] = level[b : b + 1, :]
+    for e in range(1, n_gy):
+        lvg_copy(e).start()
+
+    sub_k = lax.broadcasted_iota(jnp.int32, (SAMP, 128), 0)
+    lane_k = lax.broadcasted_iota(jnp.int32, (SAMP, 128), 1)
+    target = jnp.full((SAMP, 128), -1, jnp.int32)
+    for k in range(SAMP):
+        site = site_ref[0, k]
+        target = jnp.where(sub_k == k, (site % 2) * 64 + site // 2, target)
+    live = (target == lane_k) & (sub_k < count_ref[0, 0])
+    selector = live.astype(BF16)
 
     summed = lv_own[...]
     for e in range(1, n_gy):
@@ -442,7 +441,7 @@
 
     lv_in[0] = lv_sum[me_x]
     take_halo(0)
-    stream()
+    stream(f_ref)
 
     collide(0, 3, True)
     send_x(1)
@@ -462,9 +461,7 @@
     take_rows(0)
     rad_load.wait()
     take_halo(1)
-    stream()
-    out_copy = pltpu.make_async_copy(f_ref, adv_hbm, out_sem)
-    out_copy.start()
+    stream(adv_ref)
 
     @pl.loop(0, 16)
     def _(j):
@@ -473,7 +470,7 @@
         z0 = pl.multiple_of((j % 2) * 128, 128)
 
         def g(a, b, c):
-            return f_ref[9 * a + 3 * b + c, x, pl.ds(y0, 8), pl.ds(z0, 128)]
+            return adv_ref[9 * a + 3 * b + c, x, pl.ds(y0, 8), pl.ds(z0, 128)]
 
         put_fields(moments(g), x, y0, j % 2)
 
@@ -481,29 +478,45 @@
     take_rows(1)
     all_rows = rows[...].reshape(2 * n_gy * SAMP, 4 * ZS)
 
-    @pl.loop(0, n_gx // 4)
-    def _(t):
-        block = rad[pl.ds(t * 4, 4)].reshape(4 * OWN, 4 * ZS)
-        seen = lax.dot_general(block, all_rows, (((1,), (1,)), ((), ())), preferred_element_type=F32)
-        resp[pl.ds(t * 4, 4)] = seen.astype(BF16).reshape(4, OWN, 128)
+    seen = lax.dot_general(
+        rad[...].reshape(n_gx * OWN, 4 * ZS),
+        all_rows,
+        (((1,), (1,)), ((), ())),
+        preferred_element_type=F32,
+    )
+    resp[...] = seen.astype(BF16).reshape(n_gx, OWN, 128)
 
     @pl.loop(1, n_gx)
     def _(d):
         resp_copy(d).start()
 
     resp_in[0] = resp[me_x]
-
-    def add(d, total):
-        @pl.when(d > 0)
-        def _():
-            resp_copy(d).wait()
-
-        return total + lax.dot_general(
-            resp_in[d], one_hot[d], (((1,), (1,)), ((), ())), preferred_element_type=F32
-        )
-
-    sig_ref[...] = lax.fori_loop(0, n_gx, add, jnp.zeros((OWN, LEVELS), F32))
-    out_copy.wait()
+    total = jnp.zeros((OWN, LEVELS), F32)
+    per = max(n_gx // 4, 1)
+    for start in range(0, n_gx, per):
+        group = range(start, start + per)
+        for d in group:
+            if d > 0:
+                resp_copy(d).wait()
+        total = total + lax.dot_general(
+            jnp.concatenate([resp_in[d] for d in group], axis=1),
+            jnp.concatenate([one_hot[d] for d in group], axis=1),
+            (((1,), (1,)), ((), ())),
+            preferred_element_type=F32,
+        )
+    sig_ref[...] = total
+
+
+def finish(adv_in, sig_in, adv_out, sig_out, sem):
+    copies = [
+        pltpu.make_async_copy(adv_in.at[pl.ds(9 * a, 9)], adv_out.at[pl.ds(9 * a, 9)], sem.at[a])
+        for a in range(3)
+    ]
+    copies.append(pltpu.make_async_copy(sig_in, sig_out, sem.at[3]))
+    for copy in copies:
+        copy.start()
+    for copy in copies:
+        copy.wait()
 
 
 def per_device(populations, omega, walls, radiation, bins, counts, sample_site, sample_patch):
@@ -518,7 +531,7 @@
         pltpu.VMEM((CX, CY, NZ), F32),
         pltpu.VMEM((CX, CY, NZ), jnp.int32),
         pltpu.VMEM((n_gx, OWN, 4 * ZS), BF16),
-        pltpu.VMEM((COLUMN, n_gx), jnp.int32),
+        pltpu.VMEM((n_gx, COLUMN), jnp.int32),
         pltpu.VMEM((2, 2, 9, CY, NZ), BF16),
         pltpu.VMEM((2, 2, 9, CY, NZ), BF16),
         pltpu.VMEM((2, 2, 40, NZ), F32),
@@ -535,7 +548,6 @@
         pltpu.VMEM((n_gx, OWN, 128), BF16),
         pltpu.VMEM((n_gx, OWN, 128), BF16),
         dma((8,)),
-        dma,
         dma((2, 8)),
         dma((2, 8)),
         dma((n_gy,)),
@@ -547,27 +559,41 @@
         dma((n_gx,)),
         dma((n_gx,)),
     ]
-    return pl.pallas_call(
+    operands = (
+        sample_site.reshape(1, SAMP),
+        sample_patch.reshape(1, SAMP),
+        populations,
+        omega,
+        walls,
+        radiation.reshape(n_gx, n_gy, OWN, 4 * ZS),
+        bins.T,
+    )
+    advanced, signal = pl.pallas_call(
         functools.partial(kernel, n_gx, n_gy),
         out_shape=(
             jax.ShapeDtypeStruct((27, CX, CY, NZ), F32),
             jax.ShapeDtypeStruct((OWN, LEVELS), F32),
         ),
         in_specs=[smem] * 3 + [hbm] * 5,
-        out_specs=(hbm, vmem),
+        out_specs=(vmem, vmem),
         scratch_shapes=scratch,
-        compiler_params=pltpu.CompilerParams(collective_id=0, has_side_effects=True),
+        compiler_params=pltpu.CompilerParams(
+            collective_id=0, has_side_effects=True, vmem_limit_bytes=44 * 2**20
+        ),
         name="lattice_far_field",
-    )(
-        counts,
-        sample_site.reshape(1, SAMP),
-        sample_patch.reshape(1, SAMP),
-        populations,
-        omega,
-        walls,
-        radiation.reshape(n_gx, n_gy, OWN, 4 * ZS),
-        bins,
-    )
+    )(counts, *[pltpu.with_memory_space_constraint(x, pltpu.HBM) for x in operands])
+    return pl.pallas_call(
+        finish,
+        out_shape=(
+            jax.ShapeDtypeStruct((27, CX, CY, NZ), F32),
+            jax.ShapeDtypeStruct((OWN, LEVELS), F32),
+        ),
+        in_specs=[hbm] * 2,
+        out_specs=(hbm, hbm),
+        scratch_shapes=[dma((4,))],
+        compiler_params=pltpu.CompilerParams(vmem_limit_bytes=2**20),
+        name="write_out",
+    )(advanced, signal)
 
 
 def solution(mesh):

time: 53.3 us -> 44.5 us (0.83)
  local copies, waits for them, and re-layouts: 5.2 us -> 0 us
  Pallas kernels: 46.6 us -> 43 us
    unnamed x5 -> x0, local copies, waits for them, and re-layouts: 5.2 us -> none
    pallas_call x1, Pallas kernels: 46.6 us -> 41.8 us  [per_device(): pl.pallas_call(functools.partial(kernel, n_gx, n_gy), out_shape=(jax.Shap...]
    pallas_call x0 -> x1, Pallas kernels: none -> 1.24 us  [per_device(): pl.pallas_call(finish, out_shape=(jax.ShapeDtypeStruct((27, CX, CY, NZ),...]
where the time goes in v2:
time: 44.5 us; the launch traced here: 44.3 us
  Pallas kernels  43 us (97%)
  between operations  1.29 us (3%)
    pallas_call x1, Pallas kernels, per_device(): pl.pallas_call(functools.partial(kernel, n_gx, n_gy), out_shape=(jax.Shap...  41.8 us
    pallas_call x1, Pallas kernels, per_device(): pl.pallas_call(finish, out_shape=(jax.ShapeDtypeStruct((27, CX, CY, NZ),...  1.24 us

profile of v2, /device:TPU:1, one launch (start us, length us, event | category | flops | bytes accessed | tf_op | source)
XLA Modules:
  0.0 44.3 jit_solution(11154203893541631989)
XLA Ops:
  1.3 41.8 %lattice_far_field.1 = (f32[27,4,16,256]{3,2,1,0:T(8,128)S(1)}, f32[32,128]{1,0:T(8,128)S(1)}) custom-call(s32[1,1]{1,0:T(1,128)S(6)} %copy.10.count_ref, s32[1,16]{1,0:T(1,128)} %bitcast.6, s32[1,16]{1,0:T(1,128)} %bitcast.7, f32[27,4,16,256]{3,2,1,0:T(8,128)} %pop_hbm.1, f32[4,16,256]{2,1,0:T(8,128)} %omega_hbm.1, s32[4,16,256]{2,1,0:T(8,128)} %walls_hbm.1, ...), custom_call_target="tpu_custom_call" | custom-call | tf_op jit(solution)/shard_map/lattice_far_field/pallas_call | solution.py:571
  43.1 1.2 %write_out.1 = (f32[27,4,16,256]{3,2,1,0:T(8,128)}, f32[32,128]{1,0:T(8,128)}) custom-call(f32[27,4,16,256]{3,2,1,0:T(8,128)S(1)} %get-tuple-element.4.adv_in, f32[32,128]{1,0:T(8,128)S(1)} %get-tuple-element.5.sig_in), custom_call_target="tpu_custom_call" | custom-call | tf_op jit(solution)/shard_map/write_out/pallas_call | solution.py:585

commit v3 on v2

--- a/solution.py
+++ b/solution.py
@@ -152,6 +152,7 @@
     bins,
     xsend,
     xrecv,
+    ystage,
     ysend,
     yrecv,
     csend,
@@ -185,7 +186,7 @@
     def at_y(d):
         return lax.rem(me_y + (d + n_gy), n_gy)
 
-    layers = (0, 3, 1, 2)
+    layers = (3, 0, 1, 2)
     pop_loads = [
         pltpu.make_async_copy(pop_hbm.at[:, x], f_ref.at[:, x], load_sem.at[x]) for x in range(CX)
     ]
@@ -213,10 +214,10 @@
     for sx, sy in CORNERS:
         pl.semaphore_signal(barrier, inc=1, device_id=(at_x(sx), at_y(sy)), device_id_type=MESH)
 
-    def collide(first, step, with_fields):
-        @pl.loop(0, 8)
+    def collide(s, first, layers):
+        @pl.loop(0, 4 * layers)
         def _(j):
-            x = first + (j // 4) * step
+            x = first + j // 4
             y0 = pl.multiple_of(((j // 2) % 2) * 8, 8)
             z0 = pl.multiple_of((j % 2) * 128, 128)
 
@@ -225,10 +226,10 @@
 
             m = moments(g)
             solid = walls[x, pl.ds(y0, 8), pl.ds(z0, 128)] == 1
-            if with_fields:
+            if s == 1:
                 put_fields(m, x, y0, j % 2)
             for i, value in collided(m, omega[x, pl.ds(y0, 8), pl.ds(z0, 128)]):
-                rel[i, x + 1, pl.ds(y0 + 8, 8), pl.ds(z0, 128)] = jnp.where(solid, WALL, value)
+                rel[s, i, x + 1, pl.ds(y0 + 8, 8), pl.ds(z0, 128)] = jnp.where(solid, WALL, value)
 
     def put_fields(m, x, y0, half):
         row = pl.multiple_of(half * 64 + x * CY + y0, 8)
@@ -263,8 +264,8 @@
     def c_copy(s, corner):
         sx, sy = CORNERS[corner]
         return pltpu.make_async_remote_copy(
-            src_ref=csend.at[s, corner],
-            dst_ref=crecv.at[s, corner],
+            src_ref=csend.at[s, corner, pl.ds(0, 3)],
+            dst_ref=crecv.at[s, corner, pl.ds(0, 3)],
             send_sem=halo_send.at[s, 4 + corner],
             recv_sem=halo_recv.at[s, 4 + corner],
             device_id=(at_x(sx), at_y(sy)),
@@ -274,62 +275,84 @@
     def crossing(sy):
         return [9 * a + 3 * (sy + 1) + c for a in range(3) for c in range(3)]
 
-    def send_x(s):
-        for side in range(2):
-            for j in range(9):
-                value = rel[18 * side + j, 1 + 3 * side, pl.ds(8, CY), :]
-                xsend[s, side, j] = (value - 1.0).astype(BF16)
-            x_copy(s, side).start()
+    def send_x(s, side):
+        for j in range(9):
+            value = rel[s, 18 * side + j, 1 + 3 * side, pl.ds(8, CY), :]
+            xsend[s, side, j] = (value - 1.0).astype(BF16)
+        x_copy(s, side).start()
 
     def send_y(s):
         for side in range(2):
             edge = 8 + 15 * side
             for j, i in enumerate(crossing(2 * side - 1)):
                 for x in range(CX):
-                    ysend[s, side, 4 * j + x : 4 * j + x + 1, :] = rel[i, x + 1, edge : edge + 1, :]
+                    at = 4 * j + x
+                    ystage[side, at : at + 1, :] = rel[s, i, x + 1, edge : edge + 1, :]
+            ysend[s, side] = (ystage[side] - 1.0).astype(BF16)
             y_copy(s, side).start()
+
+    def send_corners(s):
         for corner, (sx, sy) in enumerate(CORNERS):
             edge = 23 if sy > 0 else 8
             x = 4 if sx > 0 else 1
             for c in range(3):
                 i = 9 * (sx + 1) + 3 * (sy + 1) + c
-                csend[s, corner, c : c + 1, :] = rel[i, x, edge : edge + 1, :]
+                csend[s, corner, c : c + 1, :] = rel[s, i, x, edge : edge + 1, :]
             c_copy(s, corner).start()
 
-    def take_halo(s):
+    def take_y(s):
         for side in range(2):
             y_copy(s, side).wait()
+            ystage[side] = yrecv[s, side].astype(F32) + 1.0
             edge = 7 if side == 1 else 24
             for j, i in enumerate(crossing(2 * side - 1)):
                 for x in range(CX):
-                    rel[i, x + 1, edge : edge + 1, :] = yrecv[s, side, 4 * j + x : 4 * j + x + 1, :]
+                    at = 4 * j + x
+                    rel[s, i, x + 1, edge : edge + 1, :] = ystage[side, at : at + 1, :]
+
+    def take_x(s):
         for corner, (sx, sy) in enumerate(CORNERS):
             c_copy(s, corner).wait()
             edge = 7 if sy > 0 else 24
             x = 0 if sx > 0 else 5
             for c in range(3):
                 i = 9 * (sx + 1) + 3 * (sy + 1) + c
-                rel[i, x, edge : edge + 1, :] = crecv[s, corner, c : c + 1, :]
+                rel[s, i, x, edge : edge + 1, :] = crecv[s, corner, c : c + 1, :]
         for side in range(2):
             x_copy(s, side).wait()
             for j in range(9):
-                rel[18 * side + j, 5 - 5 * side, pl.ds(8, CY), :] = (
+                rel[s, 18 * side + j, 5 - 5 * side, pl.ds(8, CY), :] = (
                     xrecv[s, side, j].astype(F32) + 1.0
                 )
 
-    def stream(to_ref):
-        @pl.loop(0, CX)
-        def _(x):
+    def stream(s, first, step):
+        to_ref = adv_ref if s == 1 else f_ref
+
+        @pl.loop(0, 2)
+        def _(j):
+            x = first + j * step
             solid = walls[x] == 1
             for i in range(27):
                 cx, cy, cz = i // 9 - 1, (i // 3) % 3 - 1, i % 3 - 1
-                source = rel[i, x + 1 - cx, pl.ds(8 - cy, CY), :]
+                source = rel[s, i, x + 1 - cx, pl.ds(8 - cy, CY), :]
                 if cz:
                     source = pltpu.roll(source, cz % NZ, 1)
                 bounced = jnp.where(
-                    source > WALL_TEST, rel[26 - i, x + 1, pl.ds(8, CY), :], source
+                    source > WALL_TEST, rel[s, 26 - i, x + 1, pl.ds(8, CY), :], source
                 )
                 to_ref[i, x] = jnp.where(solid, f_ref[i, x], bounced)
+
+    def late_fields(first, step):
+        @pl.loop(0, 8)
+        def _(j):
+            x = first + (j // 4) * step
+            y0 = pl.multiple_of(((j // 2) % 2) * 8, 8)
+            z0 = pl.multiple_of((j % 2) * 128, 128)
+
+            def g(a, b, c):
+                return adv_ref[9 * a + 3 * b + c, x, pl.ds(y0, 8), pl.ds(z0, 128)]
+
+            put_fields(moments(g), x, y0, j % 2)
 
     def send_rows(s):
         for part in range(4):
@@ -391,15 +414,18 @@
 
     omega_load.wait()
     walls_load.wait()
+    pop_loads[3].wait()
+    collide(0, 3, 1)
+    pl.semaphore_wait(barrier, n_gx - 1 + n_gy - 1 + 4)
+    send_x(0, 1)
     pop_loads[0].wait()
-    pop_loads[3].wait()
-    collide(0, 3, False)
-    pl.semaphore_wait(barrier, n_gx - 1 + n_gy - 1 + 4)
-    send_x(0)
+    collide(0, 0, 1)
+    send_x(0, 0)
     pop_loads[1].wait()
     pop_loads[2].wait()
-    collide(1, 1, False)
+    collide(0, 1, 2)
     send_y(0)
+    send_corners(0)
 
     lane = lax.broadcasted_iota(jnp.int32, (COLUMN, 128), 1)
     sub = lax.broadcasted_iota(jnp.int32, (COLUMN, 128), 0)
@@ -440,13 +466,17 @@
         lva_copy(d).start()
 
     lv_in[0] = lv_sum[me_x]
-    take_halo(0)
-    stream(f_ref)
-
-    collide(0, 3, True)
-    send_x(1)
-    collide(1, 1, True)
+    take_y(0)
+    stream(0, 1, 1)
+    collide(1, 1, 2)
+    take_x(0)
+    stream(0, 0, 3)
+    collide(1, 3, 1)
+    send_x(1, 1)
+    collide(1, 0, 1)
+    send_x(1, 0)
     send_y(1)
+    send_corners(1)
     send_rows(0)
 
     @pl.loop(0, n_gx)
@@ -460,20 +490,12 @@
 
     take_rows(0)
     rad_load.wait()
-    take_halo(1)
-    stream(adv_ref)
-
-    @pl.loop(0, 16)
-    def _(j):
-        x = j // 4
-        y0 = pl.multiple_of(((j // 2) % 2) * 8, 8)
-        z0 = pl.multiple_of((j % 2) * 128, 128)
-
-        def g(a, b, c):
-            return adv_ref[9 * a + 3 * b + c, x, pl.ds(y0, 8), pl.ds(z0, 128)]
-
-        put_fields(moments(g), x, y0, j % 2)
-
+    take_y(1)
+    stream(1, 1, 1)
+    late_fields(1, 1)
+    take_x(1)
+    stream(1, 0, 3)
+    late_fields(0, 3)
     send_rows(1)
     take_rows(1)
     all_rows = rows[...].reshape(2 * n_gy * SAMP, 4 * ZS)
@@ -491,10 +513,10 @@
         resp_copy(d).start()
 
     resp_in[0] = resp[me_x]
+    per = max(n_gx // 8, 1)
     total = jnp.zeros((OWN, LEVELS), F32)
-    per = max(n_gx // 4, 1)
-    for start in range(0, n_gx, per):
-        group = range(start, start + per)
+    for start in range(0, n_gx // 2, per):
+        group = list(range(start, start + per)) + list(range(n_gx - start - per, n_gx - start))
         for d in group:
             if d > 0:
                 resp_copy(d).wait()
@@ -527,15 +549,16 @@
     dma = pltpu.SemaphoreType.DMA
     scratch = [
         pltpu.VMEM((27, CX, CY, NZ), F32),
-        pltpu.VMEM((27, CX + 2, CY + 16, NZ), F32),
+        pltpu.VMEM((2, 27, CX + 2, CY + 16, NZ), F32),
         pltpu.VMEM((CX, CY, NZ), F32),
         pltpu.VMEM((CX, CY, NZ), jnp.int32),
         pltpu.VMEM((n_gx, OWN, 4 * ZS), BF16),
         pltpu.VMEM((n_gx, COLUMN), jnp.int32),
         pltpu.VMEM((2, 2, 9, CY, NZ), BF16),
         pltpu.VMEM((2, 2, 9, CY, NZ), BF16),
-        pltpu.VMEM((2, 2, 40, NZ), F32),
-        pltpu.VMEM((2, 2, 40, NZ), F32),
+        pltpu.VMEM((2, 9 * CX, NZ), F32),
+        pltpu.VMEM((2, 2, 9 * CX, NZ), BF16),
+        pltpu.VMEM((2, 2, 9 * CX, NZ), BF16),
         pltpu.VMEM((2, 4, 8, NZ), F32),
         pltpu.VMEM((2, 4, 8, NZ), F32),
         pltpu.VMEM((n_gx, 1, 128), F32),

time: 44.5 us -> 43.1 us (0.969)
  Pallas kernels: 43 us -> 41.7 us
    pallas_call x1, Pallas kernels: 41.8 us -> 40.4 us  [per_device(): pl.pallas_call(functools.partial(kernel, n_gx, n_gy), out_shape=(jax.Shap...]
where the time goes in v3:
time: 43.1 us; the launch traced here: 43 us
  Pallas kernels  41.7 us (97%)
  between operations  1.29 us (3%)
    pallas_call x1, Pallas kernels, per_device(): pl.pallas_call(functools.partial(kernel, n_gx, n_gy), out_shape=(jax.Shap...  40.4 us
    pallas_call x1, Pallas kernels, per_device(): pl.pallas_call(finish, out_shape=(jax.ShapeDtypeStruct((27, CX, CY, NZ),...  1.24 us

profile of v3, /device:TPU:1, one launch (start us, length us, event | category | flops | bytes accessed | tf_op | source)
XLA Modules:
  0.0 43.0 jit_solution(10066828782481980273)
XLA Ops:
  1.3 40.4 %lattice_far_field.1 = (f32[27,4,16,256]{3,2,1,0:T(8,128)S(1)}, f32[32,128]{1,0:T(8,128)S(1)}) custom-call(s32[1,1]{1,0:T(1,128)S(6)} %copy.10.count_ref, s32[1,16]{1,0:T(1,128)} %bitcast.6, s32[1,16]{1,0:T(1,128)} %bitcast.7, f32[27,4,16,256]{3,2,1,0:T(8,128)} %pop_hbm.1, f32[4,16,256]{2,1,0:T(8,128)} %omega_hbm.1, s32[4,16,256]{2,1,0:T(8,128)} %walls_hbm.1, ...), custom_call_target="tpu_custom_call" | custom-call | tf_op jit(solution)/shard_map/lattice_far_field/pallas_call | solution.py:594
  41.7 1.2 %write_out.1 = (f32[27,4,16,256]{3,2,1,0:T(8,128)}, f32[32,128]{1,0:T(8,128)}) custom-call(f32[27,4,16,256]{3,2,1,0:T(8,128)S(1)} %get-tuple-element.4.adv_in, f32[32,128]{1,0:T(8,128)S(1)} %get-tuple-element.5.sig_in), custom_call_target="tpu_custom_call" | custom-call | tf_op jit(solution)/shard_map/write_out/pallas_call | solution.py:608

commit v4 on v3

--- a/solution.py
+++ b/solution.py
@@ -455,17 +455,6 @@
     live = (target == lane_k) & (sub_k < count_ref[0, 0])
     selector = live.astype(BF16)
 
-    summed = lv_own[...]
-    for e in range(1, n_gy):
-        lvg_copy(e).wait()
-        summed = summed + lv_gy[e]
-    lv_sum[...] = summed
-
-    @pl.loop(1, n_gx)
-    def _(d):
-        lva_copy(d).start()
-
-    lv_in[0] = lv_sum[me_x]
     take_y(0)
     stream(0, 1, 1)
     collide(1, 1, 2)
@@ -479,15 +468,17 @@
     send_corners(1)
     send_rows(0)
 
-    @pl.loop(0, n_gx)
+    summed = lv_own[...]
+    for e in range(1, n_gy):
+        lvg_copy(e).wait()
+        summed = summed + lv_gy[e]
+    lv_sum[...] = summed
+
+    @pl.loop(1, n_gx)
     def _(d):
-        @pl.when(d > 0)
-        def _():
-            lva_copy(d).wait()
-
-        wanted = lax.broadcasted_iota(jnp.int32, (LEVELS, 128), 0).astype(F32)
-        one_hot[d] = (jnp.broadcast_to(lv_in[d], (LEVELS, 128)) == wanted).astype(BF16)
-
+        lva_copy(d).start()
+
+    lv_in[0] = lv_sum[me_x]
     take_rows(0)
     rad_load.wait()
     take_y(1)
@@ -513,6 +504,16 @@
         resp_copy(d).start()
 
     resp_in[0] = resp[me_x]
+
+    @pl.loop(0, n_gx)
+    def _(d):
+        @pl.when(d > 0)
+        def _():
+            lva_copy(d).wait()
+
+        wanted = lax.broadcasted_iota(jnp.int32, (LEVELS, 128), 0).astype(F32)
+        one_hot[d] = (jnp.broadcast_to(lv_in[d], (LEVELS, 128)) == wanted).astype(BF16)
+
     per = max(n_gx // 8, 1)
     total = jnp.zeros((OWN, LEVELS), F32)
     for start in range(0, n_gx // 2, per):

time: 43.1 us -> 42.1 us (0.977)
  Pallas kernels: 41.7 us -> 40.7 us
    pallas_call x1, Pallas kernels: 40.4 us -> 39.4 us  [per_device(): pl.pallas_call(functools.partial(kernel, n_gx, n_gy), out_shape=(jax.Shap...]
where the time goes in v4:
time: 42.1 us; the launch traced here: 42 us
  Pallas kernels  40.7 us (97%)
  between operations  1.29 us (3%)
    pallas_call x1, Pallas kernels, per_device(): pl.pallas_call(functools.partial(kernel, n_gx, n_gy), out_shape=(jax.Shap...  39.4 us
    pallas_call x1, Pallas kernels, per_device(): pl.pallas_call(finish, out_shape=(jax.ShapeDtypeStruct((27, CX, CY, NZ),...  1.24 us

profile of v4, /device:TPU:1, one launch (start us, length us, event | category | flops | bytes accessed | tf_op | source)
XLA Modules:
  0.0 42.0 jit_solution(6779267124821000947)
XLA Ops:
  1.3 39.4 %lattice_far_field.1 = (f32[27,4,16,256]{3,2,1,0:T(8,128)S(1)}, f32[32,128]{1,0:T(8,128)S(1)}) custom-call(s32[1,1]{1,0:T(1,128)S(6)} %copy.10.count_ref, s32[1,16]{1,0:T(1,128)} %bitcast.6, s32[1,16]{1,0:T(1,128)} %bitcast.7, f32[27,4,16,256]{3,2,1,0:T(8,128)} %pop_hbm.1, f32[4,16,256]{2,1,0:T(8,128)} %omega_hbm.1, s32[4,16,256]{2,1,0:T(8,128)} %walls_hbm.1, ...), custom_call_target="tpu_custom_call" | custom-call | tf_op jit(solution)/shard_map/lattice_far_field/pallas_call | solution.py:595
  40.7 1.2 %write_out.1 = (f32[27,4,16,256]{3,2,1,0:T(8,128)}, f32[32,128]{1,0:T(8,128)}) custom-call(f32[27,4,16,256]{3,2,1,0:T(8,128)S(1)} %get-tuple-element.4.adv_in, f32[32,128]{1,0:T(8,128)S(1)} %get-tuple-element.5.sig_in), custom_call_target="tpu_custom_call" | custom-call | tf_op jit(solution)/shard_map/write_out/pallas_call | solution.py:609

commit v5 on v4

--- a/solution.py
+++ b/solution.py
@@ -427,6 +427,10 @@
     send_y(0)
     send_corners(0)
 
+    take_y(0)
+    stream(0, 1, 1)
+    collide(1, 1, 2)
+
     lane = lax.broadcasted_iota(jnp.int32, (COLUMN, 128), 1)
     sub = lax.broadcasted_iota(jnp.int32, (COLUMN, 128), 0)
     slot_patch = jnp.full((COLUMN, 128), -1, jnp.int32)
@@ -455,9 +459,6 @@
     live = (target == lane_k) & (sub_k < count_ref[0, 0])
     selector = live.astype(BF16)
 
-    take_y(0)
-    stream(0, 1, 1)
-    collide(1, 1, 2)
     take_x(0)
     stream(0, 0, 3)
     collide(1, 3, 1)

time: 42.1 us -> 42.1 us (level)
  no operation moved by 1% of the time
where the time goes in v5:
time: 42.1 us; the launch traced here: 41.9 us
  Pallas kernels  40.6 us (96%)
  between operations  1.29 us (3%)
    pallas_call x1, Pallas kernels, per_device(): pl.pallas_call(functools.partial(kernel, n_gx, n_gy), out_shape=(jax.Shap...  39.4 us
    pallas_call x1, Pallas kernels, per_device(): pl.pallas_call(finish, out_shape=(jax.ShapeDtypeStruct((27, CX, CY, NZ),...  1.24 us

profile of v5, /device:TPU:1, one launch (start us, length us, event | category | flops | bytes accessed | tf_op | source)
XLA Modules:
  0.0 41.9 jit_solution(1519105595285392632)
XLA Ops:
  1.3 39.4 %lattice_far_field.1 = (f32[27,4,16,256]{3,2,1,0:T(8,128)S(1)}, f32[32,128]{1,0:T(8,128)S(1)}) custom-call(s32[1,1]{1,0:T(1,128)S(6)} %copy.10.count_ref, s32[1,16]{1,0:T(1,128)} %bitcast.6, s32[1,16]{1,0:T(1,128)} %bitcast.7, f32[27,4,16,256]{3,2,1,0:T(8,128)} %pop_hbm.1, f32[4,16,256]{2,1,0:T(8,128)} %omega_hbm.1, s32[4,16,256]{2,1,0:T(8,128)} %walls_hbm.1, ...), custom_call_target="tpu_custom_call" | custom-call | tf_op jit(solution)/shard_map/lattice_far_field/pallas_call | solution.py:596
  40.7 1.2 %write_out.1 = (f32[27,4,16,256]{3,2,1,0:T(8,128)}, f32[32,128]{1,0:T(8,128)}) custom-call(f32[27,4,16,256]{3,2,1,0:T(8,128)S(1)} %get-tuple-element.4.adv_in, f32[32,128]{1,0:T(8,128)S(1)} %get-tuple-element.5.sig_in), custom_call_target="tpu_custom_call" | custom-call | tf_op jit(solution)/shard_map/write_out/pallas_call | solution.py:610
